TPU v7x, 256 devices: a whole 4x4x8 slice. The times are simulated.
256 devices in a mesh: row: 32 (over y, z_lo, core), col: 8 (over x, z_hi).
Axes of the slice: x: 4, y: 4, z: 8 (z_hi: 2, z_lo: 4; z = z_hi * 4 + z_lo), core: 2. Of those that a mesh axis runs over, the one named last changes fastest.
Arguments:
- vectors: float32 [32, 524288], P(None, ('row', 'col')), may hold values from -6 to 6
- block_values: bfloat16 [65536, 128, 128], P(('row', 'col')), may hold values from -0.15625 to 0.15625
- block_rows: int32 [65536], P(('row', 'col')), may hold values from 0 to 127, as said below
- block_cols: int32 [65536], P(('row', 'col')), may hold values from 0 to 511, as said below
- block_counts: int32 [256], P(('row', 'col')), may hold values from 32 to 256, as said below
- center: float32 [1], replicated, may hold values from -0.5 to 0.5
- radius: float32 [1], replicated, may hold values from 1.5 to 3
Outputs:
- filtered: float32 [32, 524288], P(None, ('row', 'col'))
Inputs may be any that keep to these rules, and one draw needn't show every extreme that they name: `block_counts`: live slots of each device; some device fills all 256 slots. `block_rows`: Block-row inside the row group; slots may repeat a position. `block_cols`: Block-column inside the col group; slots may repeat a position.
All inputs are finite; a program needn't handle non-finite values.
Results may differ from a plain program's by a relative error of at most 0.02.
Values may be sent and summed in bfloat16 or wider, within the bound.
A program may use at most 128 MiB of HBM per device.

v0:
```python
import jax
import jax.numpy as jnp
from jax import lax
from jax.sharding import PartitionSpec as P


def block_sums(running, blocks, source, take_index, put_index, live_slots, einsum_form):
    picked = jnp.take(source, take_index, axis=1)
    products = jnp.einsum(einsum_form, blocks, picked, preferred_element_type=jnp.float32)
    products = products * live_slots[:, None, None]
    return running.at[put_index].add(products)


def region_sums(blocks, source, take_index, put_index, slot_total, segments, einsum_form):
    capacity = blocks.shape[0]
    size_block = blocks.shape[1]
    vector_count = source.shape[0]
    initial = jnp.zeros((segments, vector_count, size_block), jnp.float32)
    live_slots = (jnp.arange(capacity, dtype=jnp.int32) < slot_total).astype(jnp.float32)
    summed = block_sums(initial, blocks, source, take_index, put_index, live_slots, einsum_form)
    return jnp.transpose(summed, (1, 0, 2)).reshape(vector_count, segments * size_block)


def shards(vectors, block_values, block_rows, block_cols, block_counts, center, radius):
    size_block = block_values.shape[1]
    vector_count = vectors.shape[0]
    own_rows = vectors.shape[1]
    slot_total = block_counts[0]
    center_value = center[0]
    radius_value = radius[0]
    row_segments = lax.axis_size("col") * own_rows // size_block
    col_segments = lax.axis_size("row") * own_rows // size_block

    def apply_operator(current):
        narrow = current.astype(jnp.bfloat16)
        gathered = lax.all_gather(narrow, "row", axis=1, tiled=True)
        source = gathered.reshape(vector_count, col_segments, size_block)
        partial_rows = region_sums(
            block_values, source, block_cols, block_rows, slot_total, row_segments, "sij,ksj->ski"
        )
        forward_sum = lax.psum_scatter(
            partial_rows.astype(jnp.bfloat16), "col", scatter_dimension=1, tiled=True
        ).astype(jnp.float32)
        gathered = lax.all_gather(narrow, "col", axis=1, tiled=True)
        source = gathered.reshape(vector_count, row_segments, size_block)
        partial_cols = region_sums(
            block_values, source, block_rows, block_cols, slot_total, col_segments, "sij,ksi->skj"
        )
        mirror_sum = lax.psum_scatter(
            partial_cols.astype(jnp.bfloat16), "row", scatter_dimension=1, tiled=True
        ).astype(jnp.float32)
        return forward_sum + mirror_sum

    current = (apply_operator(vectors) - center_value * vectors) / radius_value
    following = 2.0 * (apply_operator(current) - center_value * current) / radius_value - vectors
    current = following
    return current


def solution(mesh):
    return jax.shard_map(
        shards,
        mesh=mesh,
        in_specs=(
            P(None, ("row", "col")),
            P(("row", "col"), None, None),
            P(("row", "col")),
            P(("row", "col")),
            P(("row", "col")),
            P(),
            P(),
        ),
        out_specs=P(None, ("row", "col")),
        check_vma=False,
    )
```

profile of v0, /device:TPU:1, one launch (start us, length us, event | category | flops | bytes accessed | tf_op | source)
XLA Modules:
  0.0 747.0 jit_solution(2713847587427143401)
XLA Ops:
  11.7 62.5 %all-gather.7.cloned.1.call-done = bf16[32,16384]{1,0:T(8,128)(2,1)} async-done(((bf16[32,2048]{1,0:T(8,128)(2,1)}), bf16[32,16384]{1,0:T(8,128)(2,1)}) %all-gather.7.cloned.1.call-update) | async-done | bytes 1048592 | tf_op jit(solution)/shard_map/all_gather | solution.py:44
  76.7 7.7 %convolution_multiply_fusion.2 = f32[256,32,128]{2,1,0:T(8,128)} fusion(bf16[256,128,128]{2,1,0:T(8,128)(2,1)} %param.12, bf16[256,32,128]{2,1,0:T(8,128)(2,1)S(1)} %gather_fusion.1, f32[256]{0:T(256)S(1)} %get-tuple-element.8, pred[256]{0:T(512)(128)(4,1)S(1)} %get-tuple-element.6), kind=kOutput, calls=%fused_computation.16 | convolution fusion | flops 270532608 | bytes 14681344 | tf_op jit(solution)/shard_map/sij,ksi->skj/dot_general | solution.py:9
  84.3 4.3 broadcast.28.clone
  88.6 34.1 %scatter_fusion.1 = f32[512,32,128]{2,1,0:T(8,128)} fusion(f32[512,32,128]{2,1,0:T(8,128)} %broadcast.28.clone, s32[256]{0:T(256)S(1)} %compare_select_fusion, f32[256,32,128]{2,1,0:T(8,128)} %convolution_multiply_fusion.2), kind=kCustom, calls=%fused_computation.5 | custom fusion | flops 1048576 | bytes 12583936 | tf_op jit(solution)/shard_map/scatter-add | solution.py:11
  122.8 5.8 copy_bitcast_fusion.1
  129.2 7.2 all-gather.5.cloned.1.call-done
  136.5 4.8 copy_bitcast_fusion.3
  141.3 3.2 gather_fusion
  144.5 9.8 %convolution_multiply_fusion.3 = f32[256,32,128]{2,1,0:T(8,128)} fusion(bf16[256,128,128]{2,1,0:T(8,128)(2,1)} %param.12, bf16[256,32,128]{2,1,0:T(8,128)(2,1)S(1)} %gather_fusion, f32[256]{0:T(256)S(1)} %get-tuple-element.8, pred[256]{0:T(512)(128)(4,1)S(1)} %compare_and_fusion), kind=kOutput, calls=%fused_computation.17 | convolution fusion | flops 270532608 | bytes 14681344 | tf_op jit(solution)/shard_map/sij,ksj->ski/dot_general | solution.py:9
  154.6 22.5 %scatter_fusion = f32[128,32,128]{2,1,0:T(8,128)S(1)} fusion(f32[128,32,128]{2,1,0:T(8,128)S(1)} %broadcast.25.clone, s32[256]{0:T(256)S(1)} %compare_select_fusion.1, f32[256,32,128]{2,1,0:T(8,128)} %convolution_multiply_fusion.3), kind=kCustom, calls=%fused_computation.4 | custom fusion | flops 1048576 | bytes 12583936 | tf_op jit(solution)/shard_map/scatter-add | solution.py:11
  179.5 106.4 %reduce-scatter.7.cloned.1.call-done = bf16[32,2048]{1,0:T(8,128)(2,1)} async-done(((bf16[32,65536]{1,0:T(8,128)(2,1)}), bf16[32,2048]{1,0:T(8,128)(2,1)}) %reduce-scatter.7.cloned.1.call-update) | async-done | bytes 131088 | tf_op jit(solution)/shard_map/reduce_scatter | solution.py:49
  285.9 89.5 %reduce-scatter.5.cloned.1.call-done = bf16[32,2048]{1,0:T(8,128)(2,1)} async-done(((bf16[32,16384]{1,0:T(8,128)(2,1)}), bf16[32,2048]{1,0:T(8,128)(2,1)}) %reduce-scatter.5.cloned.1.call-update) | async-done | bytes 131088 | tf_op jit(solution)/shard_map/reduce_scatter | solution.py:41
  377.9 58.4 %all-gather.11.cloned.1.call-done = bf16[32,16384]{1,0:T(8,128)(2,1)} async-done(((bf16[32,2048]{1,0:T(8,128)(2,1)}), bf16[32,16384]{1,0:T(8,128)(2,1)}) %all-gather.11.cloned.1.call-update) | async-done | bytes 1048592 | tf_op jit(solution)/shard_map/all_gather | solution.py:44
  438.8 7.7 %convolution_multiply_fusion = f32[256,32,128]{2,1,0:T(8,128)} fusion(bf16[256,128,128]{2,1,0:T(8,128)(2,1)} %param.12, bf16[256,32,128]{2,1,0:T(8,128)(2,1)S(1)} %gather_fusion.3, f32[256]{0:T(256)S(1)} %get-tuple-element.8, pred[256]{0:T(512)(128)(4,1)S(1)} %get-tuple-element.6), kind=kOutput, calls=%fused_computation.14 | convolution fusion | flops 270532608 | bytes 14681344 | tf_op jit(solution)/shard_map/sij,ksi->skj/dot_general | solution.py:9
  446.5 4.3 broadcast.28
  450.8 34.1 %scatter_fusion.3 = f32[512,32,128]{2,1,0:T(8,128)} fusion(f32[512,32,128]{2,1,0:T(8,128)} %broadcast.28, s32[256]{0:T(256)S(1)} %compare_select_fusion, f32[256,32,128]{2,1,0:T(8,128)} %convolution_multiply_fusion), kind=kCustom, calls=%fused_computation.7 | custom fusion | flops 1048576 | bytes 12583936 | tf_op jit(solution)/shard_map/scatter-add | solution.py:11
  484.9 5.8 copy_bitcast_fusion
  490.8 7.9 %all-gather.9.cloned.1.call-done = bf16[32,65536]{1,0:T(8,128)(2,1)} async-done(((bf16[32,2048]{1,0:T(8,128)(2,1)}), bf16[32,65536]{1,0:T(8,128)(2,1)}) %all-gather.9.cloned.1.call-update) | async-done | bytes 4194320 | tf_op jit(solution)/shard_map/all_gather | solution.py:36
  498.6 4.8 copy_bitcast_fusion.2
  503.5 3.2 gather_fusion.2
  506.7 9.8 %convolution_multiply_fusion.1 = f32[256,32,128]{2,1,0:T(8,128)} fusion(bf16[256,128,128]{2,1,0:T(8,128)(2,1)} %param.12, bf16[256,32,128]{2,1,0:T(8,128)(2,1)S(1)} %gather_fusion.2, f32[256]{0:T(256)S(1)} %get-tuple-element.8, pred[256]{0:T(512)(128)(4,1)S(1)} %compare_and_fusion), kind=kOutput, calls=%fused_computation.15 | convolution fusion | flops 270532608 | bytes 14681344 | tf_op jit(solution)/shard_map/sij,ksj->ski/dot_general | solution.py:9
  516.7 22.5 %scatter_fusion.2 = f32[128,32,128]{2,1,0:T(8,128)S(1)} fusion(f32[128,32,128]{2,1,0:T(8,128)S(1)} %broadcast.25, s32[256]{0:T(256)S(1)} %compare_select_fusion.1, f32[256,32,128]{2,1,0:T(8,128)} %convolution_multiply_fusion.1), kind=kCustom, calls=%fused_computation.6 | custom fusion | flops 1048576 | bytes 12583936 | tf_op jit(solution)/shard_map/scatter-add | solution.py:11
  540.3 107.2 %reduce-scatter.11.cloned.1.call-done = bf16[32,2048]{1,0:T(8,128)(2,1)} async-done(((bf16[32,65536]{1,0:T(8,128)(2,1)}), bf16[32,2048]{1,0:T(8,128)(2,1)}) %reduce-scatter.11.cloned.1.call-update) | async-done | bytes 131088 | tf_op jit(solution)/shard_map/reduce_scatter | solution.py:49
  647.5 90.8 %reduce-scatter.9.cloned.1.call-done = bf16[32,2048]{1,0:T(8,128)(2,1)} async-done(((bf16[32,16384]{1,0:T(8,128)(2,1)}), bf16[32,2048]{1,0:T(8,128)(2,1)}) %reduce-scatter.9.cloned.1.call-update) | async-done | bytes 131088 | tf_op jit(solution)/shard_map/reduce_scatter | solution.py:41
  (41 shorter events, 17.0 us)
Async XLA Ops:
  6.5 67.7 %all-gather.7.cloned.1.call-start = ((), (), s32[]{:S(2)}) async-start(), calls=%async_computation.6 | async-start | bytes 1179648 | tf_op jit(solution)/shard_map/all_gather | solution.py:44
  8.2 128.3 %all-gather.5.cloned.1.call-start = ((), (), s32[]{:S(2)}) async-start(), calls=%async_computation.4 | async-start | bytes 4325376 | tf_op jit(solution)/shard_map/all_gather | solution.py:36
  8.9 277.0 %reduce-scatter.7.cloned.1.call-start = ((), (), s32[]{:S(2)}) async-start(), calls=%async_computation.7 | async-start | bytes 4325376 | tf_op jit(solution)/shard_map/reduce_scatter | solution.py:49
  128.6 0.7 copy-start.3
  128.6 246.8 %reduce-scatter.5.cloned.1.call-start = ((), (), s32[]{:S(2)}) async-start(), calls=%async_computation.5 | async-start | bytes 1179648 | tf_op jit(solution)/shard_map/reduce_scatter | solution.py:41
  177.1 198.4 %copy-start = (f32[32,2048]{1,0:T(8,128)S(1)}, f32[32,2048]{1,0:T(8,128)}, u32[]{:S(2)}) copy-start(f32[32,2048]{1,0:T(8,128)} %param.11) | copy-start | bytes 786436
  178.2 258.2 %all-gather.11.cloned.1.call-start = ((), (), s32[]{:S(2)}) async-start(), calls=%async_computation.10 | async-start | bytes 1179648 | tf_op jit(solution)/shard_map/all_gather | solution.py:44
  377.1 121.5 %all-gather.9.cloned.1.call-start = ((), (), s32[]{:S(2)}) async-start(), calls=%async_computation.8 | async-start | bytes 4325376 | tf_op jit(solution)/shard_map/all_gather | solution.py:36
  377.7 269.8 %reduce-scatter.11.cloned.1.call-start = ((), (), s32[]{:S(2)}) async-start(), calls=%async_computation.11 | async-start | bytes 4325376 | tf_op jit(solution)/shard_map/reduce_scatter | solution.py:49
  490.7 247.6 %reduce-scatter.9.cloned.1.call-start = ((), (), s32[]{:S(2)}) async-start(), calls=%async_computation.9 | async-start | bytes 1179648 | tf_op jit(solution)/shard_map/reduce_scatter | solution.py:41
  539.2 199.1 %copy-start.1 = (bf16[32,2048]{1,0:T(8,128)(2,1)S(1)}, bf16[32,2048]{1,0:T(8,128)(2,1)}, u32[]{:S(2)}) copy-start(bf16[32,2048]{1,0:T(8,128)(2,1)} %reduce-scatter.7.cloned.1.call-done) | copy-start | bytes 393220
  539.2 199.1 %copy-start.2 = (bf16[32,2048]{1,0:T(8,128)(2,1)S(1)}, bf16[32,2048]{1,0:T(8,128)(2,1)}, u32[]{:S(2)}) copy-start(bf16[32,2048]{1,0:T(8,128)(2,1)} %reduce-scatter.5.cloned.1.call-done) | copy-start | bytes 393220
Sparse Core Ops, SparseCore 0:
  10.0 64.1 all-gather.6
  76.1 60.3 all-gather.4
  139.0 146.8 reduce-scatter.6
  289.7 85.6 reduce-scatter.4
  378.3 58.0 all-gather.10
  438.2 60.3 all-gather.8
  501.3 146.1 reduce-scatter.10
  652.0 86.3 reduce-scatter.8
where the time goes:
time: 750 us; the launch traced here: 747 us
  waiting for transfers between devices  531 us (71%)
  other arithmetic  134 us (18%)
  matrix products  35 us (5%)
  local copies, waits for them, and re-layouts  30.5 us (4%)
  between operations  15.6 us (2%)
    reduce_scatter x2, waiting for transfers between devices, apply_operator(): lax.psum_scatter(partial_cols.astype(jnp.bfloat16), 'row', scatter_dimens...  214 us
    reduce_scatter x2, waiting for transfers between devices, apply_operator(): lax.psum_scatter(partial_rows.astype(jnp.bfloat16), 'col', scatter_dimens...  180 us
    all_gather x2, waiting for transfers between devices, apply_operator(): gathered = lax.all_gather(narrow, 'col', axis=1, tiled=True)  121 us
    scatter-add x4, other arithmetic, block_sums(): return running.at[put_index].add(products)  113 us
    dot_general x4, matrix products, block_sums(): jnp.einsum(einsum_form, blocks, picked, preferred_element_type=jnp.float32)  35 us
    all_gather x2, waiting for transfers between devices, apply_operator(): gathered = lax.all_gather(narrow, 'row', axis=1, tiled=True)  15.1 us
  transfers between devices with their start and end apart: 8, of which 8 were waited for; matrix products, arithmetic and copies ran while one was open for 26% of the time, Pallas kernels for 0%

commit v1 on v0

v1 whole, which is shorter than its diff:
```python
import functools

import jax
import jax.numpy as jnp
from jax import lax
from jax.experimental import pallas as pl
from jax.experimental.pallas import tpu as pltpu
from jax.sharding import PartitionSpec as P

MESH = pl.DeviceIdType.MESH
BF16, F32 = jnp.bfloat16, jnp.float32
ANY = pl.BlockSpec(memory_space=pl.ANY)
VMEM = pl.BlockSpec(memory_space=pltpu.VMEM)
SMEM = pl.BlockSpec(memory_space=pltpu.SMEM)


class Place:
    def __init__(self):
        row, col = lax.axis_index("row"), lax.axis_index("col")
        self.row, self.col = row, col
        self.y, self.z, self.c = row // 8, (row // 2) % 4, row % 2
        self.x, self.h = col // 2, col % 2

    def row_of(self, y=None, z=None, c=None):
        y = self.y if y is None else y
        z = self.z if z is None else z
        c = self.c if c is None else c
        return (y * 4 + z) * 2 + c

    def at_y(self, step):
        return (self.row_of(y=(self.y + step) % 4), self.col)

    def at_z(self, z):
        return (self.row_of(z=z), self.col)

    def at_x(self, step):
        return (self.row, ((self.x + step) % 4) * 2 + self.h)

    def other_core(self):
        return (self.row_of(c=1 - self.c), self.col)

    def ring_z(self, step):
        zz = (self.h * 4 + self.z + 8 + step) % 8
        return (self.row_of(z=zz % 4), self.x * 2 + zz // 4)

    def half_of(self, step):
        return ((self.h * 4 + self.z + 8 + step) % 8) // 4

    def z_order(self):
        z = self.z
        return [z + 1 - 2 * (z % 2), (z + 2) % 4, 3 - z]

    def partners(self):
        found = [self.at_z(z) for z in self.z_order()]
        found += [self.at_y(1), self.at_y(3), self.at_x(1), self.at_x(3), self.other_core()]
        return found + [self.ring_z(2), self.ring_z(-2)]


class Wire:
    def __init__(self, send_sems, recv_sems):
        self.send_sems, self.recv_sems, self.copies = send_sems, recv_sems, []

    def send(self, src, dst, device):
        index = len(self.copies)
        copy = pltpu.make_async_remote_copy(
            src_ref=src,
            dst_ref=dst,
            send_sem=self.send_sems.at[index],
            recv_sem=self.recv_sems.at[index],
            device_id=device,
            device_id_type=MESH,
        )
        copy.start()
        self.copies.append(copy)
        return copy

    def drain(self):
        for copy in self.copies:
            copy.wait_send()


def greet(place):
    barrier = pltpu.get_barrier_semaphore()
    partners = place.partners()
    for partner in partners:
        pl.semaphore_signal(barrier, inc=1, device_id=partner, device_id_type=MESH)
    return barrier, len(partners)


def add_blocks(target, addend, count):
    def body(b, carry):
        target[b] = target[b] + addend[b]
        return carry

    lax.fori_loop(0, count, body, 0)


def gather_parts(place, wire, own, cols_out, rows_out, relay, local_sems):
    nb = own.shape[0]
    hf = nb // 2
    y, z, c, x, h = place.y, place.z, place.c, place.x, place.h

    def cc(yy, zz):
        return cols_out.at[pl.ds(place.row_of(y=yy, z=zz) * nb, nb)]

    def cc_half(yy, zz, part):
        return cols_out.at[pl.ds(place.row_of(y=yy, z=zz) * nb + part * hf, hf)]

    def rr(xx, hh):
        return rows_out.at[pl.ds((xx * 2 + hh) * nb, nb)]

    def rr_half(xx, hh, part):
        return rows_out.at[pl.ds((xx * 2 + hh) * nb + part * hf, hf)]

    mine_cc, mine_rr = cc(y, z), rr(x, h)
    zs = place.z_order()
    z_copies = [wire.send(own, mine_cc, place.at_z(zz)) for zz in zs]
    relay_a = wire.send(own.at[pl.ds(0, hf)], relay.at[pl.ds(0, hf)], place.ring_z(2))
    relay_b = wire.send(own.at[pl.ds(hf, hf)], relay.at[pl.ds(hf, hf)], place.ring_z(-2))
    ups = [wire.send(own, mine_cc, place.at_y(1))]
    downs = [wire.send(own, mine_cc, place.at_y(3))]
    rights = [wire.send(own, mine_rr, place.at_x(1))]
    lefts = [wire.send(own, mine_rr, place.at_x(3))]
    cores = [wire.send(own, mine_cc, place.other_core())]
    keep_cc = pltpu.make_async_copy(own, mine_cc, local_sems.at[0])
    keep_rr = pltpu.make_async_copy(own, mine_rr, local_sems.at[1])
    keep_cc.start()
    keep_rr.start()
    order = [z] + zs
    up_halves, down_halves, right_halves, left_halves = [], [], [], []

    def forward_y(k):
        ups[k].wait_recv()
        up_halves.append(wire.send(cc_half((y + 3) % 4, order[k], 0), cc_half((y + 3) % 4, order[k], 0), place.at_y(1)))
        cores.append(wire.send(cc((y + 3) % 4, order[k]), cc((y + 3) % 4, order[k]), place.other_core()))
        downs[k].wait_recv()
        down_halves.append(wire.send(cc_half((y + 1) % 4, order[k], 1), cc_half((y + 1) % 4, order[k], 1), place.at_y(3)))
        cores.append(wire.send(cc((y + 1) % 4, order[k]), cc((y + 1) % 4, order[k]), place.other_core()))

    def forward_x(k, hh):
        rights[k].wait_recv()
        right_halves.append(wire.send(rr_half((x + 3) % 4, hh, 0), rr_half((x + 3) % 4, hh, 0), place.at_x(1)))
        lefts[k].wait_recv()
        left_halves.append(wire.send(rr_half((x + 1) % 4, hh, 1), rr_half((x + 1) % 4, hh, 1), place.at_x(3)))

    def pass_on_z(k):
        z_copies[k].wait_recv()
        piece = cc(y, zs[k])
        ups.append(wire.send(piece, piece, place.at_y(1)))
        downs.append(wire.send(piece, piece, place.at_y(3)))
        cores.append(wire.send(piece, piece, place.other_core()))

    relay_a.wait_recv()
    far_a = wire.send(relay.at[pl.ds(0, hf)], rr_half(x, place.half_of(-2), 0), place.ring_z(2))
    relay_b.wait_recv()
    far_b = wire.send(relay.at[pl.ds(hf, hf)], rr_half(x, place.half_of(2), 1), place.ring_z(-2))
    pass_on_z(0)
    forward_y(0)
    forward_x(0, h)
    pass_on_z(1)
    far_a.wait_recv()
    far_b.wait_recv()
    far = rr(x, 1 - h)
    rights.append(wire.send(far, far, place.at_x(1)))
    lefts.append(wire.send(far, far, place.at_x(3)))
    forward_y(1)
    pass_on_z(2)
    forward_x(1, 1 - h)
    forward_y(2)
    forward_y(3)
    for k in range(4):
        up_halves[k].wait_recv()
        down_halves[k].wait_recv()
        piece = cc((y + 2) % 4, order[k])
        cores.append(wire.send(piece, piece, place.other_core()))
    for copy in right_halves + left_halves + cores:
        copy.wait_recv()
    keep_cc.wait()
    keep_rr.wait()


def scatter_parts(place, wire, mirror, forward, s, ca, near, d, sf, near_f, relay, v, local_sems):
    nb = v.shape[0]
    hf = nb // 2
    y, z, c, x, h = place.y, place.z, place.c, place.x, place.h
    zs = place.z_order()
    order = [zs[2], zs[1], zs[0], z]
    halves = [1 - h, h]
    bp, bm, cp, cm = near
    ep, em, gp, gm = near_f
    core_copies, locals_m, locals_f = [], [], []
    for k in range(4):
        core_copies.append(wire.send(mirror.at[:, order[k], 1 - c], ca.at[k], place.other_core()))
        local = pltpu.make_async_copy(mirror.at[:, order[k], c], s.at[k], local_sems.at[k])
        local.start()
        locals_m.append(local)
    for k in range(2):
        local = pltpu.make_async_copy(forward.at[:, halves[k]], sf.at[k], local_sems.at[4 + k])
        local.start()
        locals_f.append(local)
    first, last = pl.ds(0, hf), pl.ds(hf, hf)
    x_first = []
    for k in range(2):
        locals_f[k].wait()
        across = sf.at[k, (x + 2) % 4]
        x_first.append((
            wire.send(across.at[first], ep.at[k], place.at_x(1)),
            wire.send(across.at[last], em.at[k], place.at_x(3)),
        ))
    y_first = []
    for k in range(4):
        locals_m[k].wait()
        core_copies[k].wait_recv()
        across = (y + 2) % 4
        add_blocks(s.at[k, across], ca.at[k, across], nb)
        y_first.append((
            wire.send(s.at[k, across, first], bp.at[k], place.at_y(1)),
            wire.send(s.at[k, across, last], bm.at[k], place.at_y(3)),
        ))
        for step in (1, 3):
            add_blocks(s.at[k, (y + step) % 4], ca.at[k, (y + step) % 4], nb)
    x_second, y_second = [], []

    def second_x(k):
        x_first[k][0].wait_recv()
        add_blocks(sf.at[k, (x + 1) % 4, first], ep.at[k], hf)
        x_first[k][1].wait_recv()
        add_blocks(sf.at[k, (x + 3) % 4, last], em.at[k], hf)
        x_second.append((
            wire.send(sf.at[k, (x + 1) % 4], gp.at[k], place.at_x(1)),
            wire.send(sf.at[k, (x + 3) % 4], gm.at[k], place.at_x(3)),
        ))

    def second_y(k):
        y_first[k][0].wait_recv()
        add_blocks(s.at[k, (y + 1) % 4, first], bp.at[k], hf)
        up = wire.send(s.at[k, (y + 1) % 4], cp.at[k], place.at_y(1))
        y_first[k][1].wait_recv()
        add_blocks(s.at[k, (y + 3) % 4, last], bm.at[k], hf)
        y_second.append((up, wire.send(s.at[k, (y + 3) % 4], cm.at[k], place.at_y(3))))

    second_x(0)
    second_y(0)
    second_x(1)
    second_y(1)
    second_y(2)
    second_y(3)
    x_second[0][0].wait_recv()
    x_second[0][1].wait_recv()
    far = sf.at[0, x]

    def sum_far(b, carry):
        total = far[b].astype(F32) + gp[0, b].astype(F32) + gm[0, b].astype(F32)
        far[b] = total.astype(BF16)
        return carry

    lax.fori_loop(0, nb, sum_far, 0)
    relay_a = wire.send(far.at[first], relay.at[first], place.ring_z(2))
    relay_b = wire.send(far.at[last], relay.at[last], place.ring_z(-2))
    z_copies = []

    def third(k):
        y_second[k][0].wait_recv()
        y_second[k][1].wait_recv()
        home = s.at[k, y]

        def sum_home(b, carry):
            total = home[b].astype(F32) + ca[k, y, b].astype(F32)
            total = total + cp[k, b].astype(F32) + cm[k, b].astype(F32)
            home[b] = total.astype(BF16)
            return carry

        lax.fori_loop(0, nb, sum_home, 0)
        z_copies.append(wire.send(home, d.at[k], place.at_z(order[k])))

    third(0)
    relay_a.wait_recv()
    far_a = wire.send(relay.at[first], v.at[first], place.ring_z(2))
    relay_b.wait_recv()
    far_b = wire.send(relay.at[last], v.at[last], place.ring_z(-2))
    third(1)
    third(2)
    for copy in x_second[1] + y_second[3]:
        copy.wait_recv()
    for copy in z_copies + [far_a, far_b]:
        copy.wait_recv()

    def image(b):
        total = s[3, y, b].astype(F32) + ca[3, y, b].astype(F32)
        total = total + cp[3, b].astype(F32) + cm[3, b].astype(F32)
        total = total + d[0, b].astype(F32) + d[1, b].astype(F32) + d[2, b].astype(F32)
        total = total + sf[1, x, b].astype(F32) + gp[1, b].astype(F32) + gm[1, b].astype(F32)
        return total + v[b].astype(F32)

    return image


def gather_kernel(vectors, cols_out, rows_out, own, relay, send_sems, recv_sems, local_sems):
    place = Place()
    barrier, expected = greet(place)
    bs = own.shape[2]
    for b in range(own.shape[0]):
        own[b] = vectors[:, b * bs : (b + 1) * bs].astype(BF16)
    pl.semaphore_wait(barrier, expected)
    wire = Wire(send_sems, recv_sems)
    gather_parts(place, wire, own, cols_out, rows_out, relay, local_sems)
    wire.drain()


SCATTER_SCRATCH = 16


def scatter_scratch(nb, k, bs):
    block = (nb, k, bs)
    half = (nb // 2, k, bs)
    return [
        pltpu.VMEM((4, 4) + block, BF16),
        pltpu.VMEM((4, 4) + block, BF16),
        pltpu.VMEM((4,) + half, BF16),
        pltpu.VMEM((4,) + half, BF16),
        pltpu.VMEM((4,) + block, BF16),
        pltpu.VMEM((4,) + block, BF16),
        pltpu.VMEM((3,) + block, BF16),
        pltpu.VMEM((2, 4) + block, BF16),
        pltpu.VMEM((2,) + half, BF16),
        pltpu.VMEM((2,) + half, BF16),
        pltpu.VMEM((2,) + block, BF16),
        pltpu.VMEM((2,) + block, BF16),
        pltpu.VMEM(block, BF16),
        pltpu.VMEM(block, BF16),
        pltpu.SemaphoreType.DMA((40,)),
        pltpu.SemaphoreType.DMA((40,)),
        pltpu.SemaphoreType.DMA((6,)),
    ]


def run_scatter(place, wire, mirror, forward, scratch):
    s, ca, bp, bm, cp, cm, d, sf, ep, em, gp, gm, relay, v = scratch[:14]
    return scatter_parts(
        place, wire, mirror, forward, s, ca, (bp, bm, cp, cm), d, sf, (ep, em, gp, gm), relay, v, scratch[16]
    )


def middle_kernel(
    mirror, forward, previous, center, radius, cols_out, rows_out, current, *scratch
):
    place = Place()
    barrier, expected = greet(place)
    scatter, (own, relay, send_sems, recv_sems, local_sems) = scratch[:17], scratch[17:]
    pl.semaphore_wait(barrier, expected)
    wire = Wire(scatter[14], scatter[15])
    image = run_scatter(place, wire, mirror, forward, scatter)
    bs = own.shape[2]
    for b in range(own.shape[0]):
        part = slice(b * bs, (b + 1) * bs)
        value = (image(b) - center[0] * previous[:, part]) / radius[0]
        current[:, part] = value
        own[b] = value.astype(BF16)
    second = Wire(send_sems, recv_sems)
    gather_parts(place, second, own, cols_out, rows_out, relay, local_sems)
    wire.drain()
    second.drain()


def last_kernel(mirror, forward, previous, before, center, radius, result, *scratch):
    place = Place()
    barrier, expected = greet(place)
    pl.semaphore_wait(barrier, expected)
    wire = Wire(scratch[14], scratch[15])
    image = run_scatter(place, wire, mirror, forward, scratch)
    nb, bs = scratch[13].shape[0], scratch[13].shape[2]
    for b in range(nb):
        part = slice(b * bs, (b + 1) * bs)
        value = 2.0 * (image(b) - center[0] * previous[:, part]) / radius[0] - before[:, part]
        result[:, part] = value
    wire.drain()


def product_kernel(
    chunk, rows, cols, counts, blocks, col_source, row_source, mirror, forward, mirror_sum, forward_sum
):
    step = pl.program_id(0)
    count = counts[0]
    row_total, col_total = row_source.shape[0], col_source.shape[0]

    @pl.when(step == 0)
    def _():
        mirror_sum[...] = jnp.zeros_like(mirror_sum)
        forward_sum[...] = jnp.zeros_like(forward_sum)

    @pl.when(step * chunk < count)
    def _():
        terms = []
        for i in range(chunk):
            slot = step * chunk + i
            row, col = rows[slot], cols[slot]
            block = blocks[i]
            forward_term = lax.dot_general(
                col_source[col], block, (((1,), (1,)), ((), ())), preferred_element_type=F32
            )
            mirror_term = lax.dot_general(
                row_source[row], block, (((1,), (0,)), ((), ())), preferred_element_type=F32
            )
            live = slot < count
            terms.append((
                jnp.where(live, row, row_total), jnp.where(live, col, col_total), forward_term, mirror_term
            ))
        for row, col, forward_term, mirror_term in terms:
            forward_sum[row] += forward_term
            mirror_sum[col] += mirror_term

    @pl.when(step == pl.num_programs(0) - 1)
    def _():
        def narrow_mirror(b, carry):
            mirror[b] = mirror_sum[b].astype(BF16)
            return carry

        def narrow_forward(b, carry):
            forward[b] = forward_sum[b].astype(BF16)
            return carry

        lax.fori_loop(0, col_total, narrow_mirror, 0, unroll=8)
        lax.fori_loop(0, row_total, narrow_forward, 0, unroll=8)


CHUNK = 16


def products(block_values, rows, cols, counts, col_source, row_source):
    capacity, bs, _ = block_values.shape
    col_total, k, _ = col_source.shape
    row_total = row_source.shape[0]
    whole = lambda i, r, c, n: (0, 0, 0)
    once = pl.Buffered(1)
    return pl.pallas_call(
        functools.partial(product_kernel, CHUNK),
        out_shape=(
            jax.ShapeDtypeStruct((col_total, k, bs), BF16),
            jax.ShapeDtypeStruct((row_total, k, bs), BF16),
        ),
        grid_spec=pltpu.PrefetchScalarGridSpec(
            num_scalar_prefetch=3,
            grid=(capacity // CHUNK,),
            in_specs=[
                pl.BlockSpec((CHUNK, bs, bs), lambda i, r, c, n: (jnp.minimum(i, (n[0] - 1) // CHUNK), 0, 0)),
                pl.BlockSpec((col_total, k, bs), whole, pipeline_mode=once),
                pl.BlockSpec((row_total, k, bs), whole, pipeline_mode=once),
            ],
            out_specs=[
                pl.BlockSpec((col_total, k, bs), whole, pipeline_mode=once),
                pl.BlockSpec((row_total, k, bs), whole, pipeline_mode=once),
            ],
            scratch_shapes=[
                pltpu.VMEM((col_total + 1, k, bs), F32),
                pltpu.VMEM((row_total + 1, k, bs), F32),
            ],
        ),
        compiler_params=pltpu.CompilerParams(
            dimension_semantics=("arbitrary",), vmem_limit_bytes=40 * 2**20
        ),
    )(rows, cols, counts, block_values, col_source, row_source)


def shards(vectors, block_values, block_rows, block_cols, block_counts, center, radius):
    k, own_rows = vectors.shape
    bs = block_values.shape[1]
    nb = own_rows // bs
    row_total = lax.axis_size("col") * nb
    col_total = lax.axis_size("row") * nb
    gathered = (
        jax.ShapeDtypeStruct((col_total, k, bs), BF16),
        jax.ShapeDtypeStruct((row_total, k, bs), BF16),
    )
    whole_vectors = jax.ShapeDtypeStruct((k, own_rows), F32)
    gather_scratch = [
        pltpu.VMEM((nb, k, bs), BF16),
        pltpu.VMEM((nb, k, bs), BF16),
        pltpu.SemaphoreType.DMA((56,)),
        pltpu.SemaphoreType.DMA((56,)),
        pltpu.SemaphoreType.DMA((2,)),
    ]

    def params(index):
        return pltpu.CompilerParams(
            collective_id=index, has_side_effects=True, vmem_limit_bytes=32 * 2**20
        )

    def apart(partials):
        mirror, forward = partials
        return mirror.reshape(4, 4, 2, nb, k, bs), forward.reshape(4, 2, nb, k, bs)

    col_source, row_source = pl.pallas_call(
        gather_kernel,
        out_shape=gathered,
        in_specs=[VMEM],
        out_specs=(ANY, ANY),
        scratch_shapes=gather_scratch,
        compiler_params=params(0),
    )(vectors)
    partials = products(block_values, block_rows, block_cols, block_counts, col_source, row_source)
    col_source, row_source, current = pl.pallas_call(
        middle_kernel,
        out_shape=gathered + (whole_vectors,),
        in_specs=[ANY, ANY, VMEM, SMEM, SMEM],
        out_specs=(ANY, ANY, VMEM),
        scratch_shapes=scatter_scratch(nb, k, bs) + gather_scratch,
        compiler_params=params(1),
    )(*apart(partials), vectors, center, radius)
    partials = products(block_values, block_rows, block_cols, block_counts, col_source, row_source)
    return pl.pallas_call(
        last_kernel,
        out_shape=whole_vectors,
        in_specs=[ANY, ANY, VMEM, VMEM, SMEM, SMEM],
        out_specs=VMEM,
        scratch_shapes=scatter_scratch(nb, k, bs),
        compiler_params=params(2),
    )(*apart(partials), current, vectors, center, radius)


def solution(mesh):
    return jax.shard_map(
        shards,
        mesh=mesh,
        in_specs=(
            P(None, ("row", "col")),
            P(("row", "col"), None, None),
            P(("row", "col")),
            P(("row", "col")),
            P(("row", "col")),
            P(),
            P(),
        ),
        out_specs=P(None, ("row", "col")),
        check_vma=False,
    )
```

time: 750 us -> 180 us (0.24)
  waiting for transfers between devices: 531 us -> 0 us
  Pallas kernels: 0 us -> 174 us
  other arithmetic: 134 us -> 0 us
  matrix products: 35 us -> 0 us
  local copies, waits for them, and re-layouts: 30.5 us -> 3.02 us
  between operations: 15.6 us -> 2.04 us
    reduce_scatter x4 -> x0, waiting for transfers between devices: 394 us -> none  [the longest x2 214 us: apply_operator(): lax.psum_scatter(partial_cols.astype(jnp.bfloat16), 'row', scatter_dimens...]
    pallas_call x0 -> x5, Pallas kernels: none -> 174 us  [the longest x1 71.6 us: shards(): pl.pallas_call(middle_kernel, out_shape=gathered + (whole_vectors,), in_s...]
    all_gather x4 -> x0, waiting for transfers between devices: 136 us -> none  [the longest x2 121 us: apply_operator(): gathered = lax.all_gather(narrow, 'col', axis=1, tiled=True)]
    scatter-add x4 -> x0, other arithmetic: 113 us -> none  [block_sums(): return running.at[put_index].add(products)]
    dot_general x4 -> x0, matrix products: 35 us -> none  [block_sums(): jnp.einsum(einsum_form, blocks, picked, preferred_element_type=jnp.float32)]
    convert_element_type x6 -> x0, other arithmetic: 17 us -> none  [the longest x2 11.6 us: apply_operator(): partial_cols.astype(jnp.bfloat16)]
    reshape x4 -> x0, local copies, waits for them, and re-layouts: 12.5 us -> none  [the longest x2 9.67 us: apply_operator(): source = gathered.reshape(vector_count, col_segments, size_block)]
    another operation x4 -> x0, local copies, waits for them, and re-layouts: 9.1 us -> none
  transfers between devices with their start and end apart: 8 -> 0, of which waited for: 8 -> 0; matrix products, arithmetic and copies ran while one was open for 26% -> 0% of each run, Pallas kernels for 0% -> 0%
where the time goes in v1:
time: 180 us; the launch traced here: 179 us
  Pallas kernels  174 us (97%)
  local copies, waits for them, and re-layouts  3.02 us (2%)
  between operations  2.04 us (1%)
    pallas_call x1, Pallas kernels, shards(): pl.pallas_call(middle_kernel, out_shape=gathered + (whole_vectors,), in_s...  71.6 us
    pallas_call x1, Pallas kernels, shards(): pl.pallas_call(gather_kernel, out_shape=gathered, in_specs=[VMEM], out_sp...  43.9 us
    pallas_call x1, Pallas kernels, shards(): pl.pallas_call(last_kernel, out_shape=whole_vectors, in_specs=[ANY, ANY,...  37.8 us
    pallas_call x2, Pallas kernels, products(): pl.pallas_call(functools.partial(product_kernel, CHUNK), out_shape=(jax.S...  20.9 us

profile of v1, /device:TPU:1, one launch (start us, length us, event | category | flops | bytes accessed | tf_op | source)
XLA Modules:
  0.0 179.2 jit_solution(7076371982175106669)
XLA Ops:
  1.9 0.0 copy-start
  2.0 0.9 copy-done
  2.9 43.9 %shard_map.73 = (bf16[512,32,128]{2,1,0:T(8,128)(2,1)S(1)}, bf16[128,32,128]{2,1,0:T(8,128)(2,1)S(1)}) custom-call(f32[32,2048]{1,0:T(8,128)S(1)} %copy-done), custom_call_target="tpu_custom_call" | custom-call | tf_op jit(solution)/shard_map/pallas_call | solution.py:492
  46.8 0.0 copy-start.2
  46.8 0.7 copy-done.2
  47.5 0.0 copy-start.4
  47.5 0.7 copy-done.4
  48.2 0.0 copy-start.1
  48.2 10.4 %shard_map.74 = (bf16[512,32,128]{2,1,0:T(8,128)(2,1)S(1)}, bf16[128,32,128]{2,1,0:T(8,128)(2,1)S(1)}) custom-call(s32[256]{0:T(256)S(1)} %copy-done.2, s32[256]{0:T(256)S(1)} %copy-done.4, s32[1]{0:T(128)S(6)} %copy.9.counts, bf16[256,128,128]{2,1,0:T(8,128)(2,1)} %blocks.3, bf16[512,32,128]{2,1,0:T(8,128)(2,1)S(1)} %get-tuple-element.14.col_source, ...), custom_call_target="tpu_custom_call" | custom-call | tf_op jit(solution)/shard_map/pallas_call | solution.py:435
  58.6 0.0 copy-start.3
  58.6 0.0 copy-start.5
  58.6 0.0 copy-done.1
  58.6 71.6 %shard_map.75 = (bf16[512,32,128]{2,1,0:T(8,128)(2,1)S(1)}, bf16[128,32,128]{2,1,0:T(8,128)(2,1)S(1)}, f32[32,2048]{1,0:T(8,128)S(1)}) custom-call(bf16[4,4,2,16,32,128]{5,4,3,2,1,0:T(8,128)(2,1)S(1)} %bitcast.5, bf16[4,2,16,32,128]{4,3,2,1,0:T(8,128)(2,1)S(1)} %bitcast.7, f32[32,2048]{1,0:T(8,128)S(1)} %copy-done.1, f32[1]{0:T(128)S(6)} %copy.10.center, ...), custom_call_target="tpu_custom_call" | custom-call | tf_op jit(solution)/shard_map/pallas_call | solution.py:501
  130.2 0.0 copy-done.3
  130.2 0.0 copy-done.5
  130.2 10.4 %shard_map.76 = (bf16[512,32,128]{2,1,0:T(8,128)(2,1)S(1)}, bf16[128,32,128]{2,1,0:T(8,128)(2,1)S(1)}) custom-call(s32[256]{0:T(256)S(1)} %copy-done.3, s32[256]{0:T(256)S(1)} %copy-done.5, s32[1]{0:T(128)S(6)} %copy.9.counts, bf16[256,128,128]{2,1,0:T(8,128)(2,1)} %blocks.3, bf16[512,32,128]{2,1,0:T(8,128)(2,1)S(1)} %get-tuple-element.18.col_source, ...), custom_call_target="tpu_custom_call" | custom-call | tf_op jit(solution)/shard_map/pallas_call | solution.py:435
  140.7 37.8 %shard_map.77 = f32[32,2048]{1,0:T(8,128)S(1)} custom-call(bf16[4,4,2,16,32,128]{5,4,3,2,1,0:T(8,128)(2,1)S(1)} %bitcast.4, bf16[4,2,16,32,128]{4,3,2,1,0:T(8,128)(2,1)S(1)} %bitcast.6, f32[32,2048]{1,0:T(8,128)S(1)} %get-tuple-element.22.previous, f32[32,2048]{1,0:T(8,128)S(1)} %copy-done.1, f32[1]{0:T(128)S(6)} %copy.10.center, f32[1]{0:T(128)S(6)} %copy.11.radius), custom_call_target="tpu_custom_call" | custom-call | tf_op jit(solution)/shard_map/pallas_call | solution.py:510
  178.5 0.7 copy.12
Async XLA Ops:
  1.9 1.0 copy-start
  46.8 0.7 copy-start.2
  47.5 0.7 copy-start.4
  48.2 10.5 %copy-start.1 = (f32[32,2048]{1,0:T(8,128)S(1)}, f32[32,2048]{1,0:T(8,128)}, u32[]{:S(2)}) copy-start(f32[32,2048]{1,0:T(8,128)} %before.1) | copy-start | bytes 786436
  58.6 71.6 %copy-start.3 = (s32[256]{0:T(256)S(1)}, s32[256]{0:T(256)}, u32[]{:S(2)}) copy-start(s32[256]{0:T(256)} %rows.3) | copy-start | bytes 3076
  58.6 71.6 %copy-start.5 = (s32[256]{0:T(256)S(1)}, s32[256]{0:T(256)}, u32[]{:S(2)}) copy-start(s32[256]{0:T(256)} %cols.3) | copy-start | bytes 3076

commit v2 on v0

v2 whole, which is shorter than its diff:
```python
import functools

import jax
import jax.numpy as jnp
from jax import lax
from jax.experimental import pallas as pl
from jax.experimental.pallas import tpu as pltpu
from jax.sharding import PartitionSpec as P

MESH = pl.DeviceIdType.MESH
BF16, F32 = jnp.bfloat16, jnp.float32
ANY = pl.BlockSpec(memory_space=pl.ANY)
VMEM = pl.BlockSpec(memory_space=pltpu.VMEM)
SMEM = pl.BlockSpec(memory_space=pltpu.SMEM)
GATHER_COPIES, SCATTER_COPIES = 48, 32
UNROLL = 16


class Place:
    def __init__(self):
        row, col = lax.axis_index("row"), lax.axis_index("col")
        self.row, self.col = row, col
        self.y, self.z, self.c = row // 8, (row // 2) % 4, row % 2
        self.x, self.h = col // 2, col % 2
        z = self.z
        self.inner = (z == 1) | (z == 2)
        self.pair = z + 1 - 2 * (z % 2)
        self.near_z = 2 - z // 2
        self.far_z = 3 - 3 * (z // 2)

    def row_of(self, y=None, z=None, c=None):
        y = self.y if y is None else y
        z = self.z if z is None else z
        c = self.c if c is None else c
        return (y * 4 + z) * 2 + c

    def at_y(self, step):
        return (self.row_of(y=(self.y + step) % 4), self.col)

    def at_z(self, z):
        return (self.row_of(z=z), self.col)

    def at_x(self, step):
        return (self.row, ((self.x + step) % 4) * 2 + self.h)

    def other_core(self):
        return (self.row_of(c=1 - self.c), self.col)

    def across_z(self):
        return (self.row, self.x * 2 + 1 - self.h)

    def partners(self):
        z = self.z
        found = [self.other_core(), self.at_y(1), self.at_y(3), self.at_x(1), self.at_x(3)]
        found += [self.at_z(self.pair), self.at_z((z + 2) % 4), self.at_z(3 - z)]
        return found + [self.across_z()]


class Wire:
    def __init__(self, send_sems, recv_sems):
        self.send_sems, self.recv_sems = send_sems, recv_sems
        self.started, self.count = [], 0

    def slot(self):
        self.count += 1
        return self.count - 1

    def send(self, src, dst, device, recv=None, when=None):
        index = self.slot()
        copy = pltpu.make_async_remote_copy(
            src_ref=src,
            dst_ref=dst,
            send_sem=self.send_sems.at[index],
            recv_sem=self.recv_sems.at[index if recv is None else recv],
            device_id=device,
            device_id_type=MESH,
        )
        if when is None:
            copy.start()
        else:
            pl.when(when)(copy.start)
        self.started.append((copy, when))
        return copy

    def drain(self):
        for copy, when in self.started:
            if when is None:
                copy.wait_send()
            else:
                pl.when(when)(copy.wait_send)


def gather_parts(place, wire, cols_out, rows_out, nb, mirror_steps):
    hf = nb // 2
    y, z, c, x, h = place.y, place.z, place.c, place.x, place.h

    def cc(yy, zz, part=None):
        start, size = (0, nb) if part is None else (part * hf, hf)
        return cols_out.at[pl.ds(place.row_of(y=yy, z=zz) * nb + start, size)]

    def rr(xx, hh, part=None):
        start, size = (0, nb) if part is None else (part * hf, hf)
        return rows_out.at[pl.ds((xx * 2 + hh) * nb + start, size)]

    same = lambda ref, device, **kw: wire.send(ref, ref, device, **kw)
    mid, pair = place.at_z(3 - z), place.at_z(place.pair)
    order = [z, place.pair, place.near_z, place.far_z]
    ups, downs, rights, lefts, cores = [], [], [], [], []
    up_halves, down_halves, right_halves, left_halves = [], [], [], []

    def along_y(k):
        piece = cc(y, order[k])
        ups.append(same(piece, place.at_y(1)))
        downs.append(same(piece, place.at_y(3)))
        cores.append(same(piece, place.other_core()))

    def along_x(hh):
        rights.append(same(rr(x, hh), place.at_x(1)))
        lefts.append(same(rr(x, hh), place.at_x(3)))

    def forward_y(k):
        low, high = (y + 3) % 4, (y + 1) % 4
        ups[k].wait_recv()
        up_halves.append(same(cc(low, order[k], 0), place.at_y(1)))
        cores.append(same(cc(low, order[k]), place.other_core()))
        downs[k].wait_recv()
        down_halves.append(same(cc(high, order[k], 1), place.at_y(3)))
        cores.append(same(cc(high, order[k]), place.other_core()))

    def forward_x(k, hh):
        rights[k].wait_recv()
        right_halves.append(same(rr((x + 3) % 4, hh, 0), place.at_x(1)))
        lefts[k].wait_recv()
        left_halves.append(same(rr((x + 1) % 4, hh, 1), place.at_x(3)))

    def last_y(k):
        up_halves[k].wait_recv()
        down_halves[k].wait_recv()
        cores.append(same(cc((y + 2) % 4, order[k]), place.other_core()))

    mine, near_slot, far_slot = cc(y, z), wire.slot(), wire.slot()
    from_pair = same(mine, pair)
    from_near = same(mine, mid, recv=near_slot, when=place.inner)
    along_y(0)
    along_x(h)
    far = same(rr(x, h), place.across_z())
    from_pair.wait_recv()
    from_far = same(cc(y, place.pair), mid, recv=far_slot, when=place.inner)
    along_y(1)
    from_near.wait_recv()
    same(cc(y, place.near_z), pair, recv=near_slot, when=place.inner)
    along_y(2)
    forward_y(0)
    forward_x(0, h)
    from_far.wait_recv()
    same(cc(y, place.far_z), pair, recv=far_slot, when=place.inner)
    along_y(3)
    forward_y(1)
    far.wait_recv()
    along_x(1 - h)
    forward_x(1, 1 - h)
    forward_y(2)
    for copy in right_halves + left_halves:
        copy.wait_recv()
    mirror_steps[0]()
    forward_y(3)
    last_y(0)
    last_y(1)
    mirror_steps[1]()
    last_y(2)
    mirror_steps[2]()
    last_y(3)
    mirror_steps[3]()
    for copy in cores:
        copy.wait_recv()


def scatter_parts(place, wire, here, local, nb, last_of_col, last_of_row, forward_steps):
    ca, bp, bm, cp, cm, d, ep, em, gp, gm, v = here
    mirror_sums, forward_sums, mo, s, sf = local
    hf = nb // 2
    y, z, c, x, h = place.y, place.z, place.c, place.x, place.h
    order = [3 - z, (z + 2) % 4, place.pair, z]
    halves = [1 - h, h]
    first, last = pl.ds(0, hf), pl.ds(hf, hf)
    core_copies, y_first, y_second, x_first, x_second, z_copies = [], [], [], [], [], []

    def blocks(count, body):
        def step(b, carry):
            body(b)
            return carry

        lax.fori_loop(0, count, step, 0, unroll=4)

    def mirror_part(k, yy, core, b):
        return mirror_sums[last_of_col(((yy * 4 + order[k]) * 2 + core) * nb + b)]

    def add(target, addend):
        def body(b):
            target[b] = target[b] + addend[b]

        blocks(hf, body)

    def to_core(k):
        for yy in range(4):

            def body(b):
                mo[k, yy, b] = mirror_part(k, yy, 1 - c, b).astype(BF16)

            blocks(nb, body)
        core_copies.append(wire.send(mo.at[k], ca.at[k], place.other_core()))

    def own(k, yy):
        def body(b):
            s[k, yy, b] = (mirror_part(k, yy, c, b) + ca[k, yy, b].astype(F32)).astype(BF16)

        blocks(nb, body)

    def first_y(k):
        across = (y + 2) % 4
        core_copies[k].wait_recv()
        own(k, across)
        y_first.append((
            wire.send(s.at[k, across, first], bp.at[k], place.at_y(1)),
            wire.send(s.at[k, across, last], bm.at[k], place.at_y(3)),
        ))
        own(k, (y + 1) % 4)
        own(k, (y + 3) % 4)

    def second_y(k):
        y_first[k][0].wait_recv()
        add(s.at[k, (y + 1) % 4, first], bp.at[k])
        up = wire.send(s.at[k, (y + 1) % 4], cp.at[k], place.at_y(1))
        y_first[k][1].wait_recv()
        add(s.at[k, (y + 3) % 4, last], bm.at[k])
        y_second.append((up, wire.send(s.at[k, (y + 3) % 4], cm.at[k], place.at_y(3))))

    def home(k, b):
        total = mirror_part(k, y, c, b) + ca[k, y, b].astype(F32)
        return total + cp[k, b].astype(F32) + cm[k, b].astype(F32)

    def third(k):
        y_second[k][0].wait_recv()
        y_second[k][1].wait_recv()

        def body(b):
            s[k, y, b] = home(k, b).astype(BF16)

        blocks(nb, body)
        z_copies.append(wire.send(s.at[k, y], d.at[k], place.at_z(order[k])))

    def first_x(k):
        for xx in range(4):

            def body(b):
                sf[k, xx, b] = forward_sums[last_of_row((xx * 2 + halves[k]) * nb + b)].astype(BF16)

            blocks(nb, body)
        across = (x + 2) % 4
        x_first.append((
            wire.send(sf.at[k, across, first], ep.at[k], place.at_x(1)),
            wire.send(sf.at[k, across, last], em.at[k], place.at_x(3)),
        ))

    def second_x(k):
        x_first[k][0].wait_recv()
        add(sf.at[k, (x + 1) % 4, first], ep.at[k])
        right = wire.send(sf.at[k, (x + 1) % 4], gp.at[k], place.at_x(1))
        x_first[k][1].wait_recv()
        add(sf.at[k, (x + 3) % 4, last], em.at[k])
        x_second.append((right, wire.send(sf.at[k, (x + 3) % 4], gm.at[k], place.at_x(3))))

    def across_z():
        x_second[0][0].wait_recv()
        x_second[0][1].wait_recv()

        def body(b):
            total = sf[0, x, b].astype(F32) + gp[0, b].astype(F32) + gm[0, b].astype(F32)
            sf[0, x, b] = total.astype(BF16)

        blocks(nb, body)
        return wire.send(sf.at[0, x], v, place.across_z())

    for k in range(4):
        to_core(k)
    first_y(0)
    first_y(1)
    forward_steps[0]()
    second_y(0)
    first_y(2)
    forward_steps[1]()
    second_y(1)
    first_y(3)
    forward_steps[2]()
    second_y(2)
    third(0)
    forward_steps[3]()
    first_x(0)
    first_x(1)
    second_y(3)
    third(1)
    second_x(0)
    second_x(1)
    far = across_z()
    third(2)
    for copy in x_second[1] + y_second[3] + tuple(z_copies) + (far,):
        copy.wait_recv()

    def image(b):
        total = home(3, b)
        total = total + d[0, b].astype(F32) + d[1, b].astype(F32) + d[2, b].astype(F32)
        total = total + sf[1, x, b].astype(F32) + gp[1, b].astype(F32) + gm[1, b].astype(F32)
        return total + v[b].astype(F32)

    return image


REMOTE = 13


def filter_kernel(
    vectors, tables, center, radius, blocks_hbm, result, blocks, mirror_sums, forward_sums, mo, s, sf, current,
    *rest,
):
    place = Place()
    barrier = pltpu.get_barrier_semaphore()
    partners = place.partners()
    for partner in partners:
        pl.semaphore_signal(barrier, inc=1, device_id=partner, device_id_type=MESH)
    products = [rest[:REMOTE], rest[REMOTE : 2 * REMOTE]]
    gather_sems, scatter_sems, block_sem = rest[2 * REMOTE : 2 * REMOTE + 4], rest[2 * REMOTE + 4 : -1], rest[-1]
    capacity, bs = blocks.shape[0], blocks.shape[1]
    nb = vectors.shape[1] // bs
    col_total, row_total = products[0][0].shape[0], products[0][1].shape[0]
    fetch = pltpu.make_async_copy(blocks_hbm, blocks, block_sem)
    fetch.start()
    k = vectors.shape[0]
    mirror_sums[capacity] = jnp.zeros((k, bs), F32)
    forward_sums[capacity] = jnp.zeros((k, bs), F32)
    row_at = lambda i: tables[i]
    col_at = lambda i: tables[capacity + i]
    before_in_row = lambda i: tables[2 * capacity + i]
    before_in_col = lambda i: tables[3 * capacity + i]
    last_of_row = lambda i: tables[4 * capacity + i]
    last_of_col = lambda i: tables[4 * capacity + row_total + i]
    span = capacity // 4

    def steps(source, source_at, before, sums, contract):
        def part(first):
            def body(i, carry):
                start = first + i * UNROLL
                terms = [
                    lax.dot_general(
                        source[source_at(start + u)],
                        blocks[start + u],
                        (((1,), (contract,)), ((), ())),
                        preferred_element_type=F32,
                    )
                    for u in range(UNROLL)
                ]
                for u in range(UNROLL):
                    sums[start + u] = terms[u] + sums[before(start + u)]
                return carry

            lax.fori_loop(0, span // UNROLL, body, 0)

        return [functools.partial(part, i * span) for i in range(4)]

    def put_own(cols_out, rows_out, b, value):
        narrow = value.astype(BF16)
        cols_out[place.row * nb + b] = narrow
        rows_out[place.col * nb + b] = narrow

    for b in range(nb):
        put_own(products[0][0], products[0][1], b, vectors[:, b * bs : (b + 1) * bs])
    pl.semaphore_wait(barrier, len(partners))
    for p in range(2):
        cols_in, rows_in = products[p][:2]
        mirror_steps = steps(rows_in, row_at, before_in_col, mirror_sums, 0)
        forward_steps = steps(cols_in, col_at, before_in_row, forward_sums, 1)
        if p == 0:
            first_step = mirror_steps[0]

            def fetched(first_step=first_step):
                fetch.wait()
                first_step()

            mirror_steps[0] = fetched
        gather = Wire(gather_sems[2 * p], gather_sems[2 * p + 1])
        gather_parts(place, gather, cols_in, rows_in, nb, mirror_steps)
        scatter = Wire(scatter_sems[2 * p], scatter_sems[2 * p + 1])
        image = scatter_parts(
            place, scatter, products[p][2:], (mirror_sums, forward_sums, mo, s, sf), nb, last_of_col, last_of_row,
            forward_steps,
        )
        for b in range(nb):
            part = slice(b * bs, (b + 1) * bs)
            if p == 0:
                value = (image(b) - center[0] * vectors[:, part]) / radius[0]
                current[:, part] = value
                put_own(products[1][0], products[1][1], b, value)
            else:
                value = 2.0 * (image(b) - center[0] * current[:, part]) / radius[0] - vectors[:, part]
                result[:, part] = value
        gather.drain()
        scatter.drain()


def slot_tables(rows, cols, counts, row_total, col_total):
    capacity = rows.shape[0]
    slots = jnp.arange(capacity, dtype=jnp.int32)
    live = slots < counts[0]

    def latest(keys, queries, limits):
        hits = (keys[None, :] == queries[:, None]) & (slots[None, :] < limits[:, None]) & live[None, :]
        found = jnp.max(jnp.where(hits, slots[None, :], -1), axis=1)
        return jnp.where(found < 0, capacity, found)

    def whole(keys, total):
        return latest(keys, jnp.arange(total, dtype=jnp.int32), jnp.full((total,), capacity, jnp.int32))

    return jnp.concatenate([
        rows, cols, latest(rows, rows, slots), latest(cols, cols, slots), whole(rows, row_total), whole(cols, col_total)
    ])


def shards(vectors, block_values, block_rows, block_cols, block_counts, center, radius):
    k, own_rows = vectors.shape
    capacity, bs, _ = block_values.shape
    nb = own_rows // bs
    row_total = lax.axis_size("col") * nb
    col_total = lax.axis_size("row") * nb
    tables = slot_tables(block_rows, block_cols, block_counts, row_total, col_total)
    whole, half = (nb, k, bs), (nb // 2, k, bs)
    remote = [
        pltpu.VMEM((col_total, k, bs), BF16),
        pltpu.VMEM((row_total, k, bs), BF16),
        pltpu.VMEM((4, 4) + whole, BF16),
        pltpu.VMEM((4,) + half, BF16),
        pltpu.VMEM((4,) + half, BF16),
        pltpu.VMEM((4,) + whole, BF16),
        pltpu.VMEM((4,) + whole, BF16),
        pltpu.VMEM((3,) + whole, BF16),
        pltpu.VMEM((2,) + half, BF16),
        pltpu.VMEM((2,) + half, BF16),
        pltpu.VMEM((2,) + whole, BF16),
        pltpu.VMEM((2,) + whole, BF16),
        pltpu.VMEM(whole, BF16),
    ]
    return pl.pallas_call(
        filter_kernel,
        out_shape=jax.ShapeDtypeStruct((k, own_rows), F32),
        in_specs=[VMEM, SMEM, SMEM, SMEM, ANY],
        out_specs=VMEM,
        scratch_shapes=[
            pltpu.VMEM((capacity, bs, bs), BF16),
            pltpu.VMEM((capacity + 1, k, bs), F32),
            pltpu.VMEM((capacity + 1, k, bs), F32),
            pltpu.VMEM((4, 4) + whole, BF16),
            pltpu.VMEM((4, 4) + whole, BF16),
            pltpu.VMEM((2, 4) + whole, BF16),
            pltpu.VMEM((k, own_rows), F32),
        ]
        + remote * 2
        + [pltpu.SemaphoreType.DMA((GATHER_COPIES,))] * 4
        + [pltpu.SemaphoreType.DMA((SCATTER_COPIES,))] * 4
        + [pltpu.SemaphoreType.DMA],
        compiler_params=pltpu.CompilerParams(
            collective_id=0, has_side_effects=True, vmem_limit_bytes=56 * 2**20
        ),
        name="filter",
    )(vectors, tables, center, radius, block_values)


def solution(mesh):
    return jax.shard_map(
        shards,
        mesh=mesh,
        in_specs=(
            P(None, ("row", "col")),
            P(("row", "col"), None, None),
            P(("row", "col")),
            P(("row", "col")),
            P(("row", "col")),
            P(),
            P(),
        ),
        out_specs=P(None, ("row", "col")),
        check_vma=False,
    )
```

time: 750 us -> 145 us (0.19)
  waiting for transfers between devices: 531 us -> 0 us
  Pallas kernels: 0 us -> 135 us
  other arithmetic: 134 us -> 2.74 us
  matrix products: 35 us -> 0 us
  local copies, waits for them, and re-layouts: 30.5 us -> 3.63 us
  between operations: 15.6 us -> 2.01 us
    reduce_scatter x4 -> x0, waiting for transfers between devices: 394 us -> none  [the longest x2 214 us: apply_operator(): lax.psum_scatter(partial_cols.astype(jnp.bfloat16), 'row', scatter_dimens...]
    all_gather x4 -> x0, waiting for transfers between devices: 136 us -> none  [the longest x2 121 us: apply_operator(): gathered = lax.all_gather(narrow, 'col', axis=1, tiled=True)]
    pallas_call x0 -> x1, Pallas kernels: none -> 135 us  [shards(): pl.pallas_call(filter_kernel, out_shape=jax.ShapeDtypeStruct((k, own_rows...]
    scatter-add x4 -> x0, other arithmetic: 113 us -> none  [block_sums(): return running.at[put_index].add(products)]
    dot_general x4 -> x0, matrix products: 35 us -> none  [block_sums(): jnp.einsum(einsum_form, blocks, picked, preferred_element_type=jnp.float32)]
    convert_element_type x6 -> x0, other arithmetic: 17 us -> none  [the longest x2 11.6 us: apply_operator(): partial_cols.astype(jnp.bfloat16)]
    reshape x4 -> x0, local copies, waits for them, and re-layouts: 12.5 us -> none  [the longest x2 9.67 us: apply_operator(): source = gathered.reshape(vector_count, col_segments, size_block)]
    another operation x4 -> x0, local copies, waits for them, and re-layouts: 9.1 us -> none
  transfers between devices with their start and end apart: 8 -> 0, of which waited for: 8 -> 0; matrix products, arithmetic and copies ran while one was open for 26% -> 0% of each run, Pallas kernels for 0% -> 0%
where the time goes in v2:
time: 145 us; the launch traced here: 144 us
  Pallas kernels  135 us (93%)
  local copies, waits for them, and re-layouts  3.63 us (3%)
  other arithmetic  2.74 us (2%)
  between operations  2.01 us (1%)
    pallas_call x1, Pallas kernels, shards(): pl.pallas_call(filter_kernel, out_shape=jax.ShapeDtypeStruct((k, own_rows...  135 us
    unnamed x5, local copies, waits for them, and re-layouts  3.63 us

profile of v2, /device:TPU:1, one launch (start us, length us, event | category | flops | bytes accessed | tf_op | source)
XLA Modules:
  0.0 143.7 jit_solution(9695937068683619153)
XLA Ops:
  2.0 0.8 select_reduce_fusion.3
  2.8 0.9 select_reduce_fusion
  3.6 1.0 select_reduce_fusion.1
  4.7 0.7 constant_dynamic-update-slice_fusion.5
  5.4 0.7 constant_dynamic-update-slice_fusion.4
  6.1 0.0 copy-start
  6.1 0.6 copy-done
  6.7 135.3 %filter.1 = f32[32,2048]{1,0:T(8,128)} custom-call(f32[32,2048]{1,0:T(8,128)} %vectors.1, s32[1664]{0:T(1024)} %copy-done, f32[1]{0:T(128)S(6)} %copy.16.center, f32[1]{0:T(128)S(6)} %copy.17.radius, bf16[256,128,128]{2,1,0:T(8,128)(2,1)} %blocks_hbm.1), custom_call_target="tpu_custom_call" | custom-call | tf_op jit(solution)/shard_map/filter/pallas_call | solution.py:450
  142.0 1.7 %copy.18 = f32[32,2048]{1,0:T(8,128)} copy(f32[32,2048]{1,0:T(8,128)} %filter.1) | data formatting | bytes 524288
  (6 shorter events, 0.0 us)
Async XLA Ops:
  6.1 0.6 copy-start

commit v3 on v0

v3 whole, which is shorter than its diff:
```python
import functools

import jax
import jax.numpy as jnp
from jax import lax
from jax.experimental import pallas as pl
from jax.experimental.pallas import tpu as pltpu
from jax.sharding import PartitionSpec as P

MESH = pl.DeviceIdType.MESH
BF16, F32 = jnp.bfloat16, jnp.float32
ANY = pl.BlockSpec(memory_space=pl.ANY)
VMEM = pl.BlockSpec(memory_space=pltpu.VMEM)
SMEM = pl.BlockSpec(memory_space=pltpu.SMEM)
COPIES, PARTS, UNROLL = 80, 4, 16


class Place:
    def __init__(self):
        row, col = lax.axis_index("row"), lax.axis_index("col")
        self.row, self.col = row, col
        self.y, self.z, self.c = row // 8, (row // 2) % 4, row % 2
        self.x, self.h = col // 2, col % 2
        z = self.z
        self.inner = (z == 1) | (z == 2)
        self.pair = z + 1 - 2 * (z % 2)
        self.near_z = 2 - z // 2
        self.far_z = 3 - 3 * (z // 2)

    def row_of(self, y=None, z=None, c=None):
        y = self.y if y is None else y
        z = self.z if z is None else z
        c = self.c if c is None else c
        return (y * 4 + z) * 2 + c

    def at_y(self, step):
        return (self.row_of(y=(self.y + step) % 4), self.col)

    def at_z(self, z):
        return (self.row_of(z=z), self.col)

    def at_x(self, step):
        return (self.row, ((self.x + step) % 4) * 2 + self.h)

    def other_core(self):
        return (self.row_of(c=1 - self.c), self.col)

    def across_z(self):
        return (self.row, self.x * 2 + 1 - self.h)

    def partners(self):
        z = self.z
        found = [self.other_core(), self.at_y(1), self.at_y(3), self.at_x(1), self.at_x(3)]
        found += [self.at_z(self.pair), self.at_z((z + 2) % 4), self.at_z(3 - z)]
        return found + [self.across_z()]


class Wire:
    def __init__(self, send_sems, recv_sems):
        self.send_sems, self.recv_sems = send_sems, recv_sems
        self.started, self.count = [], 0

    def slot(self):
        self.count += 1
        return self.count - 1

    def send(self, src, dst, device, recv=None, when=None):
        index = self.slot()
        copy = pltpu.make_async_remote_copy(
            src_ref=src,
            dst_ref=dst,
            send_sem=self.send_sems.at[index],
            recv_sem=self.recv_sems.at[index if recv is None else recv],
            device_id=device,
            device_id_type=MESH,
        )
        if when is None:
            copy.start()
        else:
            pl.when(when)(copy.start)
        self.started.append((copy, when))
        return copy

    def drain(self):
        for copy, when in self.started:
            if when is None:
                copy.wait_send()
            else:
                pl.when(when)(copy.wait_send)


SCRIPT = [
    "P", "N", "y0", "Z", "x0", "c0", "|", "wp", "F", "y1", "c1", "wn", "n>", "y2", "Y0", "X0", "wz", "x1",
    "c2", "C0", "wf", "f>", "y3", "Y1", "X1", "c3", "C1", "Y2", "C2", "H", "M0", "Y3", "C3", "M1", "L0", "D0",
    "L1", "D1", "M2", "L2", "D2", "M3", "A0", "A1", "A2", "A3", "B0", "B1", "L3", "D3", "B2", "B3", "K", "S0",
    "E0", "S1", "E1", "S2", "S3", "q0", "q1", "E2", "T0", "r0", "E3", "T1", "r1", "T2", "v", "W",
]


class Product:
    def __init__(self, place, wire, nb, remote, local, last_of_row, last_of_col, mirror_part, forward_part):
        self.place, self.wire, self.nb, self.hf = place, wire, nb, nb // 2
        self.cols, self.rows = remote[:2]
        self.ca, self.bp, self.bm, self.cp, self.cm, self.d, self.ep, self.em, self.gp, self.gm, self.v = remote[2:]
        self.mirror_sums, self.forward_sums, self.mo, self.s, self.sf = local
        self.last_of_row, self.last_of_col = last_of_row, last_of_col
        self.mirror_part, self.forward_part = mirror_part, forward_part
        self.near_slot, self.far_slot = wire.slot(), wire.slot()
        self.pieces = [place.z, place.pair, place.near_z, place.far_z]
        self.sums = [3 - place.z, (place.z + 2) % 4, place.pair, place.z]
        self.halves = [1 - place.h, place.h]
        self.made, self.cores = {}, []

    def run(self, codes):
        for code in codes:
            name, index = (code[:-1], int(code[-1])) if code[-1].isdigit() else (code, None)
            step = getattr(self, STEPS[name])
            step() if index is None else step(index)


    def cc(self, y, z, start=0, size=None):
        size = self.nb if size is None else size
        return self.cols.at[pl.ds(self.place.row_of(y=y, z=z) * self.nb + start, size)]

    def rr(self, x, h, start=0, size=None):
        size = self.nb if size is None else size
        return self.rows.at[pl.ds((x * 2 + h) * self.nb + start, size)]

    def same(self, key, ref, device, **options):
        self.made[key] = self.wire.send(ref, ref, device, **options)

    def arrived(self, *keys):
        for key in keys:
            self.made[key].wait_recv()

    def to_pair(self):
        self.same("pair", self.cc(self.place.y, self.place.z), self.place.at_z(self.place.pair))

    def to_middle(self):
        p = self.place
        self.same("near", self.cc(p.y, p.z), p.at_z(3 - p.z), recv=self.near_slot, when=p.inner)

    def pair_to_middle(self):
        p = self.place
        self.same("far", self.cc(p.y, p.pair), p.at_z(3 - p.z), recv=self.far_slot, when=p.inner)

    def near_to_pair(self):
        p = self.place
        self.same("near2", self.cc(p.y, p.near_z), p.at_z(p.pair), recv=self.near_slot, when=p.inner)

    def far_to_pair(self):
        p = self.place
        self.same("far2", self.cc(p.y, p.far_z), p.at_z(p.pair), recv=self.far_slot, when=p.inner)

    def wait_pair(self):
        self.arrived("pair")

    def wait_near(self):
        self.arrived("near")

    def wait_far(self):
        self.arrived("far")

    def along_y(self, k):
        p = self.place
        piece = self.cc(p.y, self.pieces[k])
        self.same(("up", k), piece, p.at_y(1))
        self.same(("down", k), piece, p.at_y(3))

    def core(self, y, k):
        piece = self.cc(y % 4, self.pieces[k])
        self.cores.append(self.wire.send(piece, piece, self.place.other_core()))

    def core_own(self, k):
        self.core(self.place.y, k)

    def core_next(self, k):
        self.core(self.place.y + 3, k)
        self.core(self.place.y + 1, k)

    def core_across(self, k):
        self.core(self.place.y + 2, k)

    def forward_y(self, k):
        p, hf = self.place, self.hf
        self.arrived(("up", k))
        self.same(("up half", k), self.cc((p.y + 3) % 4, self.pieces[k], 0, hf), p.at_y(1))
        self.arrived(("down", k))
        self.same(("down half", k), self.cc((p.y + 1) % 4, self.pieces[k], hf, hf), p.at_y(3))

    def wait_y(self, k):
        self.arrived(("up half", k), ("down half", k))

    def across(self):
        p = self.place
        self.same("z", self.rr(p.x, p.h), p.across_z())

    def wait_across(self):
        self.arrived("z")

    def along_x(self, i):
        p = self.place
        piece = self.rr(p.x, self.halves[1 - i])
        self.same(("right", i), piece, p.at_x(1))
        self.same(("left", i), piece, p.at_x(3))

    def forward_x(self, i):
        p, hf, h = self.place, self.hf, self.halves[1 - i]
        self.arrived(("right", i))
        self.same(("right half", i), self.rr((p.x + 3) % 4, h, 0, hf), p.at_x(1))
        self.arrived(("left", i))
        self.same(("left half", i), self.rr((p.x + 1) % 4, h, hf, hf), p.at_x(3))

    def wait_x(self):
        for i in range(2):
            self.arrived(("right half", i), ("left half", i))

    def wait_cores(self):
        for copy in self.cores:
            copy.wait_recv()


    def blocks(self, count, body):
        def step(b, carry):
            body(b)
            return carry

        lax.fori_loop(0, count, step, 0, unroll=4)

    def mirror_of(self, k, y, core, b):
        return self.mirror_sums[self.last_of_col(((y * 4 + self.sums[k]) * 2 + core) * self.nb + b)]

    def add(self, target, addend):
        def body(b):
            target[b] = target[b] + addend[b]

        self.blocks(self.hf, body)

    def send(self, key, src, dst, device):
        self.made[key] = self.wire.send(src, dst, device)

    def to_core(self, k):
        for y in range(4):

            def body(b):
                self.mo[k, y, b] = self.mirror_of(k, y, 1 - self.place.c, b).astype(BF16)

            self.blocks(self.nb, body)
        self.send(("core", k), self.mo.at[k], self.ca.at[k], self.place.other_core())

    def own(self, k, y):
        def body(b):
            mine = self.mirror_of(k, y, self.place.c, b)
            self.s[k, y, b] = (mine + self.ca[k, y, b].astype(F32)).astype(BF16)

        self.blocks(self.nb, body)

    def first_y(self, k):
        p, hf = self.place, self.hf
        across = (p.y + 2) % 4
        self.arrived(("core", k))
        self.own(k, across)
        self.send(("b up", k), self.s.at[k, across, pl.ds(0, hf)], self.bp.at[k], p.at_y(1))
        self.send(("b down", k), self.s.at[k, across, pl.ds(hf, hf)], self.bm.at[k], p.at_y(3))
        self.own(k, (p.y + 1) % 4)
        self.own(k, (p.y + 3) % 4)

    def second_y(self, k):
        p, hf = self.place, self.hf
        up, down = (p.y + 1) % 4, (p.y + 3) % 4
        self.arrived(("b up", k))
        self.add(self.s.at[k, up, pl.ds(0, hf)], self.bp.at[k])
        self.send(("c up", k), self.s.at[k, up], self.cp.at[k], p.at_y(1))
        self.arrived(("b down", k))
        self.add(self.s.at[k, down, pl.ds(hf, hf)], self.bm.at[k])
        self.send(("c down", k), self.s.at[k, down], self.cm.at[k], p.at_y(3))

    def home(self, k, b):
        total = self.mirror_of(k, self.place.y, self.place.c, b) + self.ca[k, self.place.y, b].astype(F32)
        return total + self.cp[k, b].astype(F32) + self.cm[k, b].astype(F32)

    def third_z(self, k):
        self.arrived(("c up", k), ("c down", k))
        target = self.s.at[k, self.place.y]

        def body(b):
            target[b] = self.home(k, b).astype(BF16)

        self.blocks(self.nb, body)
        self.send(("d", k), target, self.d.at[k], self.place.at_z(self.sums[k]))

    def first_x(self, k):
        p, hf = self.place, self.hf
        for x in range(4):

            def body(b):
                at = (x * 2 + self.halves[k]) * self.nb + b
                self.sf[k, x, b] = self.forward_sums[self.last_of_row(at)].astype(BF16)

            self.blocks(self.nb, body)
        across = (p.x + 2) % 4
        self.send(("e right", k), self.sf.at[k, across, pl.ds(0, hf)], self.ep.at[k], p.at_x(1))
        self.send(("e left", k), self.sf.at[k, across, pl.ds(hf, hf)], self.em.at[k], p.at_x(3))

    def second_x(self, k):
        p, hf = self.place, self.hf
        right, left = (p.x + 1) % 4, (p.x + 3) % 4
        self.arrived(("e right", k))
        self.add(self.sf.at[k, right, pl.ds(0, hf)], self.ep.at[k])
        self.send(("g right", k), self.sf.at[k, right], self.gp.at[k], p.at_x(1))
        self.arrived(("e left", k))
        self.add(self.sf.at[k, left, pl.ds(hf, hf)], self.em.at[k])
        self.send(("g left", k), self.sf.at[k, left], self.gm.at[k], p.at_x(3))

    def third_x(self):
        self.arrived(("g right", 0), ("g left", 0))
        target = self.sf.at[0, self.place.x]

        def body(b):
            total = target[b].astype(F32) + self.gp[0, b].astype(F32) + self.gm[0, b].astype(F32)
            target[b] = total.astype(BF16)

        self.blocks(self.nb, body)
        self.send("v", target, self.v, self.place.across_z())

    def wait_sums(self):
        self.arrived(("c up", 3), ("c down", 3), ("g right", 1), ("g left", 1))
        self.arrived(("d", 0), ("d", 1), ("d", 2), "v")

    def image(self, b):
        total = self.home(3, b)
        total = total + self.d[0, b].astype(F32) + self.d[1, b].astype(F32) + self.d[2, b].astype(F32)
        total = total + self.sf[1, self.place.x, b].astype(F32)
        total = total + self.gp[1, b].astype(F32) + self.gm[1, b].astype(F32)
        return total + self.v[b].astype(F32)


STEPS = dict(
    P="to_pair", N="to_middle", F="pair_to_middle", wp="wait_pair", wn="wait_near", wf="wait_far", y="along_y",
    c="core_own", C="core_next", D="core_across", Y="forward_y", L="wait_y", Z="across", wz="wait_across",
    x="along_x", X="forward_x", H="wait_x", K="wait_cores", M="mirror_part", S="forward_part", A="to_core",
    B="first_y", E="second_y", T="third_z", q="first_x", r="second_x", v="third_x", W="wait_sums",
)
STEPS["n>"], STEPS["f>"] = "near_to_pair", "far_to_pair"


REMOTE = 13


def filter_kernel(
    vectors, row_keys, col_keys, row_at, col_at, counts, center, radius, blocks_hbm, result,
    blocks, mirror_sums, forward_sums, mo, s, sf, current, found, tables, *rest,
):
    place = Place()
    barrier = pltpu.get_barrier_semaphore()
    partners = place.partners()
    for partner in partners:
        pl.semaphore_signal(barrier, inc=1, device_id=partner, device_id_type=MESH)
    products = [rest[:REMOTE], rest[REMOTE : 2 * REMOTE]]
    sems, block_sem, table_sem = rest[2 * REMOTE : -2], rest[-2], rest[-1]
    capacity, bs = blocks.shape[0], blocks.shape[1]
    nb = vectors.shape[1] // bs
    col_total, row_total = products[0][0].shape[0], products[0][1].shape[0]
    fetch = pltpu.make_async_copy(blocks_hbm, blocks, block_sem)
    fetch.start()
    k = vectors.shape[0]
    mirror_sums[capacity] = jnp.zeros((k, bs), F32)
    forward_sums[capacity] = jnp.zeros((k, bs), F32)
    before_in_row = lambda i: tables[0, i]
    before_in_col = lambda i: tables[0, capacity + i]
    last_of_row = lambda i: tables[0, 2 * capacity + i]
    last_of_col = lambda i: tables[0, 2 * capacity + row_total + i]
    span = capacity // PARTS

    def part_of(source, source_at, before, sums, contract):
        def part(index):
            first = index * span

            def body(i, carry):
                start = first + i * UNROLL
                terms = [
                    lax.dot_general(
                        source[source_at[start + u]],
                        blocks[start + u],
                        (((1,), (contract,)), ((), ())),
                        preferred_element_type=F32,
                    )
                    for u in range(UNROLL)
                ]
                for u in range(UNROLL):
                    sums[start + u] = terms[u] + sums[before(start + u)]
                return carry

            lax.fori_loop(0, span // UNROLL, body, 0)

        return part

    def put_own(cols_out, rows_out, b, value):
        narrow = value.astype(BF16)
        cols_out[place.row * nb + b] = narrow
        rows_out[place.col * nb + b] = narrow

    def make_tables():
        square = (capacity, capacity)
        down, along = lax.broadcasted_iota(jnp.int32, square, 0), lax.broadcasted_iota(jnp.int32, square, 1)
        count = counts[0]
        offset = 0

        def store(hits, size):
            nonlocal offset
            slots = lax.broadcasted_iota(jnp.int32, (capacity, size), 0)
            latest = jnp.max(jnp.where(hits, slots, -1), axis=0, keepdims=True)
            found[:, offset : offset + size] = jnp.where(latest < 0, capacity, latest)
            offset += size

        keys_down = []
        for keys in (row_keys, col_keys):
            spread = jnp.broadcast_to(keys[...], square)
            down_keys = jnp.sum(jnp.where(down == along, spread, 0), axis=1, keepdims=True)
            keys_down.append(down_keys)
            store((down_keys == spread) & (down < along) & (down < count), capacity)
        for down_keys, total in zip(keys_down, (row_total, col_total)):
            wanted = lax.broadcasted_iota(jnp.int32, (capacity, total), 1)
            live = lax.broadcasted_iota(jnp.int32, (capacity, total), 0) < count
            store((down_keys == wanted) & live, total)
        copy = pltpu.make_async_copy(found, tables, table_sem)
        copy.start()
        copy.wait()

    for b in range(nb):
        put_own(products[0][0], products[0][1], b, vectors[:, b * bs : (b + 1) * bs])
    pl.semaphore_wait(barrier, len(partners))
    for p in range(2):
        mirror_part = part_of(products[p][1], row_at, before_in_col, mirror_sums, 0)
        forward_part = part_of(products[p][0], col_at, before_in_row, forward_sums, 1)
        wire = Wire(sems[2 * p], sems[2 * p + 1])
        product = Product(
            place, wire, nb, products[p], (mirror_sums, forward_sums, mo, s, sf), last_of_row, last_of_col,
            mirror_part, forward_part,
        )
        tables_at = SCRIPT.index("|")
        product.run(SCRIPT[:tables_at])
        if p == 0:
            make_tables()
            fetch.wait()
        product.run(SCRIPT[tables_at + 1 :])
        for b in range(nb):
            part = slice(b * bs, (b + 1) * bs)
            if p == 0:
                value = (product.image(b) - center[0] * vectors[:, part]) / radius[0]
                current[:, part] = value
                put_own(products[1][0], products[1][1], b, value)
            else:
                value = 2.0 * (product.image(b) - center[0] * current[:, part]) / radius[0] - vectors[:, part]
                result[:, part] = value
        wire.drain()


def shards(vectors, block_values, block_rows, block_cols, block_counts, center, radius):
    k, own_rows = vectors.shape
    capacity, bs, _ = block_values.shape
    nb = own_rows // bs
    row_total = lax.axis_size("col") * nb
    col_total = lax.axis_size("row") * nb
    whole, half = (nb, k, bs), (nb // 2, k, bs)
    remote = [
        pltpu.VMEM((col_total, k, bs), BF16),
        pltpu.VMEM((row_total, k, bs), BF16),
        pltpu.VMEM((4, 4) + whole, BF16),
        pltpu.VMEM((4,) + half, BF16),
        pltpu.VMEM((4,) + half, BF16),
        pltpu.VMEM((4,) + whole, BF16),
        pltpu.VMEM((4,) + whole, BF16),
        pltpu.VMEM((3,) + whole, BF16),
        pltpu.VMEM((2,) + half, BF16),
        pltpu.VMEM((2,) + half, BF16),
        pltpu.VMEM((2,) + whole, BF16),
        pltpu.VMEM((2,) + whole, BF16),
        pltpu.VMEM(whole, BF16),
    ]
    return pl.pallas_call(
        filter_kernel,
        out_shape=jax.ShapeDtypeStruct((k, own_rows), F32),
        in_specs=[VMEM, VMEM, VMEM, SMEM, SMEM, SMEM, SMEM, SMEM, ANY],
        out_specs=VMEM,
        scratch_shapes=[
            pltpu.VMEM((capacity, bs, bs), BF16),
            pltpu.VMEM((capacity + 1, k, bs), F32),
            pltpu.VMEM((capacity + 1, k, bs), F32),
            pltpu.VMEM((4, 4) + whole, BF16),
            pltpu.VMEM((4, 4) + whole, BF16),
            pltpu.VMEM((2, 4) + whole, BF16),
            pltpu.VMEM((k, own_rows), F32),
            pltpu.VMEM((1, 2 * capacity + row_total + col_total), jnp.int32),
            pltpu.SMEM((1, 2 * capacity + row_total + col_total), jnp.int32),
        ]
        + remote * 2
        + [pltpu.SemaphoreType.DMA((COPIES,))] * 4
        + [pltpu.SemaphoreType.DMA] * 2,
        compiler_params=pltpu.CompilerParams(
            collective_id=0, has_side_effects=True, vmem_limit_bytes=56 * 2**20
        ),
        name="filter",
    )(
        vectors, block_rows.reshape(1, capacity), block_cols.reshape(1, capacity), block_rows, block_cols,
        block_counts, center, radius, block_values,
    )


def solution(mesh):
    return jax.shard_map(
        shards,
        mesh=mesh,
        in_specs=(
            P(None, ("row", "col")),
            P(("row", "col"), None, None),
            P(("row", "col")),
            P(("row", "col")),
            P(("row", "col")),
            P(),
            P(),
        ),
        out_specs=P(None, ("row", "col")),
        check_vma=False,
    )
```

time: 750 us -> 135 us (0.18)
  waiting for transfers between devices: 531 us -> 0 us
  other arithmetic: 134 us -> 0 us
  Pallas kernels: 0 us -> 132 us
  matrix products: 35 us -> 0 us
  local copies, waits for them, and re-layouts: 30.5 us -> 1.67 us
  between operations: 15.6 us -> 1.95 us
    reduce_scatter x4 -> x0, waiting for transfers between devices: 394 us -> none  [the longest x2 214 us: apply_operator(): lax.psum_scatter(partial_cols.astype(jnp.bfloat16), 'row', scatter_dimens...]
    all_gather x4 -> x0, waiting for transfers between devices: 136 us -> none  [the longest x2 121 us: apply_operator(): gathered = lax.all_gather(narrow, 'col', axis=1, tiled=True)]
    pallas_call x0 -> x1, Pallas kernels: none -> 132 us  [shards(): pl.pallas_call(filter_kernel, out_shape=jax.ShapeDtypeStruct((k, own_rows...]
    scatter-add x4 -> x0, other arithmetic: 113 us -> none  [block_sums(): return running.at[put_index].add(products)]
    dot_general x4 -> x0, matrix products: 35 us -> none  [block_sums(): jnp.einsum(einsum_form, blocks, picked, preferred_element_type=jnp.float32)]
    convert_element_type x6 -> x0, other arithmetic: 17 us -> none  [the longest x2 11.6 us: apply_operator(): partial_cols.astype(jnp.bfloat16)]
    reshape x4 -> x0, local copies, waits for them, and re-layouts: 12.5 us -> none  [the longest x2 9.67 us: apply_operator(): source = gathered.reshape(vector_count, col_segments, size_block)]
    another operation x4 -> x0, local copies, waits for them, and re-layouts: 9.1 us -> none
  transfers between devices with their start and end apart: 8 -> 0, of which waited for: 8 -> 0; matrix products, arithmetic and copies ran while one was open for 26% -> 0% of each run, Pallas kernels for 0% -> 0%
where the time goes in v3:
time: 135 us
  Pallas kernels  132 us (98%)
  between operations  1.95 us (1%)
  local copies, waits for them, and re-layouts  1.67 us (1%)
    pallas_call x1, Pallas kernels, shards(): pl.pallas_call(filter_kernel, out_shape=jax.ShapeDtypeStruct((k, own_rows...  132 us

profile of v3, /device:TPU:1, one launch (start us, length us, event | category | flops | bytes accessed | tf_op | source)
XLA Modules:
  0.0 135.2 jit_solution(10782876099208720057)
XLA Ops:
  1.9 131.6 %filter.1 = f32[32,2048]{1,0:T(8,128)} custom-call(f32[32,2048]{1,0:T(8,128)} %vectors.1, s32[1,256]{1,0:T(1,128)} %bitcast.2, s32[1,256]{1,0:T(1,128)} %bitcast.3, s32[256]{0:T(256)} %row_at.1, s32[256]{0:T(256)} %col_at.1, s32[1]{0:T(128)S(6)} %copy.9.counts, f32[1]{0:T(128)S(6)} %copy.10.center, f32[1]{0:T(128)S(6)} %copy.11.radius, ...), custom_call_target="tpu_custom_call" | custom-call | tf_op jit(solution)/shard_map/filter/pallas_call | solution.py:481
  133.5 1.7 %copy.12 = f32[32,2048]{1,0:T(8,128)} copy(f32[32,2048]{1,0:T(8,128)} %filter.1) | data formatting | bytes 524288

commit v4 on v3

--- a/solution.py
+++ b/solution.py
@@ -12,7 +12,7 @@
 ANY = pl.BlockSpec(memory_space=pl.ANY)
 VMEM = pl.BlockSpec(memory_space=pltpu.VMEM)
 SMEM = pl.BlockSpec(memory_space=pltpu.SMEM)
-COPIES, PARTS, UNROLL = 80, 4, 16
+COPIES, PARTS, UNROLL = 80, 4, 32
 
 
 class Place:
@@ -92,8 +92,8 @@
 SCRIPT = [
     "P", "N", "y0", "Z", "x0", "c0", "|", "wp", "F", "y1", "c1", "wn", "n>", "y2", "Y0", "X0", "wz", "x1",
     "c2", "C0", "wf", "f>", "y3", "Y1", "X1", "c3", "C1", "Y2", "C2", "H", "M0", "Y3", "C3", "M1", "L0", "D0",
-    "L1", "D1", "M2", "L2", "D2", "M3", "A0", "A1", "A2", "A3", "B0", "B1", "L3", "D3", "B2", "B3", "K", "S0",
-    "E0", "S1", "E1", "S2", "S3", "q0", "q1", "E2", "T0", "r0", "E3", "T1", "r1", "T2", "v", "W",
+    "L1", "D1", "M2", "L2", "D2", "M3", "A0", "A1", "A2", "A3", "B0", "B1", "L3", "D3", "B2", "B3", "K", "E0",
+    "S0", "E1", "S1", "S2", "T0", "E2", "S3", "q0", "q1", "T1", "E3", "r0", "T2", "r1", "v", "W",
 ]
 
 

time: 135 us -> 136 us (level)
  no operation moved by 1% of the time
where the time goes in v4:
time: 136 us
  Pallas kernels  133 us (98%)
  between operations  1.95 us (1%)
  local copies, waits for them, and re-layouts  1.67 us (1%)
    pallas_call x1, Pallas kernels, shards(): pl.pallas_call(filter_kernel, out_shape=jax.ShapeDtypeStruct((k, own_rows...  133 us

profile of v4, /device:TPU:1, one launch (start us, length us, event | category | flops | bytes accessed | tf_op | source)
XLA Modules:
  0.0 136.2 jit_solution(2996959752514482517)
XLA Ops:
  1.9 132.6 %filter.1 = f32[32,2048]{1,0:T(8,128)} custom-call(f32[32,2048]{1,0:T(8,128)} %vectors.1, s32[1,256]{1,0:T(1,128)} %bitcast.2, s32[1,256]{1,0:T(1,128)} %bitcast.3, s32[256]{0:T(256)} %row_at.1, s32[256]{0:T(256)} %col_at.1, s32[1]{0:T(128)S(6)} %copy.9.counts, f32[1]{0:T(128)S(6)} %copy.10.center, f32[1]{0:T(128)S(6)} %copy.11.radius, ...), custom_call_target="tpu_custom_call" | custom-call | tf_op jit(solution)/shard_map/filter/pallas_call | solution.py:481
  134.5 1.7 %copy.12 = f32[32,2048]{1,0:T(8,128)} copy(f32[32,2048]{1,0:T(8,128)} %filter.1) | data formatting | bytes 524288

commit v5 on v3

--- a/solution.py
+++ b/solution.py
@@ -12,7 +12,7 @@
 ANY = pl.BlockSpec(memory_space=pl.ANY)
 VMEM = pl.BlockSpec(memory_space=pltpu.VMEM)
 SMEM = pl.BlockSpec(memory_space=pltpu.SMEM)
-COPIES, PARTS, UNROLL = 80, 4, 16
+COPIES, PARTS, UNROLL = 80, 4, 32
 
 
 class Place:

time: 135 us -> 133 us (0.985)
  Pallas kernels: 132 us -> 128 us
    pallas_call x1, Pallas kernels: 132 us -> 128 us  [shards(): pl.pallas_call(filter_kernel, out_shape=jax.ShapeDtypeStruct((k, own_rows...]
where the time goes in v5:
time: 133 us; the launch traced here: 132 us
  Pallas kernels  128 us (96%)
  between operations  1.95 us (1%)
  local copies, waits for them, and re-layouts  1.67 us (1%)
    pallas_call x1, Pallas kernels, shards(): pl.pallas_call(filter_kernel, out_shape=jax.ShapeDtypeStruct((k, own_rows...  128 us

profile of v5, /device:TPU:1, one launch (start us, length us, event | category | flops | bytes accessed | tf_op | source)
XLA Modules:
  0.0 131.9 jit_solution(18378882294568261988)
XLA Ops:
  1.9 128.3 %filter.1 = f32[32,2048]{1,0:T(8,128)} custom-call(f32[32,2048]{1,0:T(8,128)} %vectors.1, s32[1,256]{1,0:T(1,128)} %bitcast.2, s32[1,256]{1,0:T(1,128)} %bitcast.3, s32[256]{0:T(256)} %row_at.1, s32[256]{0:T(256)} %col_at.1, s32[1]{0:T(128)S(6)} %copy.9.counts, f32[1]{0:T(128)S(6)} %copy.10.center, f32[1]{0:T(128)S(6)} %copy.11.radius, ...), custom_call_target="tpu_custom_call" | custom-call | tf_op jit(solution)/shard_map/filter/pallas_call | solution.py:481
  130.2 1.7 %copy.12 = f32[32,2048]{1,0:T(8,128)} copy(f32[32,2048]{1,0:T(8,128)} %filter.1) | data formatting | bytes 524288
